TPU v7x, 512 devices: a whole 4x8x8 slice. The times are simulated.
512 devices in a mesh: wide: 64 (over y, z_hi, core), batch: 8 (over z_lo, x).
Axes of the slice: x: 4, y: 8, z: 8 (z_hi: 4, z_lo: 2; z = z_hi * 2 + z_lo), core: 2. Of those that a mesh axis runs over, the one named last changes fastest.
Arguments:
- integrals: bfloat16 [1536, 64, 640], P('wide'), may hold values from -0.8984375 to 0.8984375
- vir_coeff: bfloat16 [640, 512], P(None, 'batch'), may hold values from -0.25 to 0.25
- occ_energy: float32 [64], replicated, may hold values from -1.6 to -0.4
- vir_energy: float32 [512], replicated, may hold values from 0.2 to 3
- kappas: float32 [8], replicated, may hold values from 0.1 to 3
Outputs:
- density: bfloat16 [8, 64, 512, 1536], P(None, 'wide', 'batch')
All inputs are finite; a program needn't handle non-finite values.
Results may differ from a plain program's by a relative error of at most 0.0051.
Values may be sent and summed in bfloat16 or wider, within the bound.
A program may use at most 64 MiB of HBM per device.

v0:
```python
import jax
import jax.numpy as jnp
from jax import lax
from jax.sharding import PartitionSpec as P

HALF = 2


def from_behind(shard, axis, by):
    peers = lax.axis_size(axis)
    return lax.ppermute(shard, axis, [(i, (i + by) % peers) for i in range(peers)])


def pair_density(own_slice, partner, own_energy, partner_energy, row_energy, vir_energy, kappas):
    coulomb = lax.dot_general(
        own_slice, partner, (((0,), (0,)), ((), ())), preferred_element_type=jnp.float32
    )
    denominator = row_energy[:, None] + vir_energy[None, :] - own_energy - partner_energy
    damping = 1.0 - jnp.exp(-kappas[:, None, None] * denominator[None])
    amplitude = (-coulomb[None] * (damping * damping) / denominator[None]).astype(jnp.bfloat16)
    flat = amplitude.reshape(-1, amplitude.shape[2])
    density = lax.dot_general(
        flat, partner, (((1,), (1,)), ((), ())), preferred_element_type=jnp.float32
    )
    return density.reshape(kappas.shape[0], own_slice.shape[1], partner.shape[0])


def on_device(integrals, vir_coeff, occ_energy, vir_energy, kappas):
    aux_local, occ_count, basis = integrals.shape
    vir_local = vir_coeff.shape[1]
    batch_index = lax.axis_index("batch")
    wide_index = lax.axis_index("wide")
    flat_ints = integrals.reshape(aux_local * occ_count, basis)
    row_energy = lax.dynamic_slice_in_dim(vir_energy, batch_index * vir_local, vir_local, 0)
    own_energy = lax.dynamic_slice_in_dim(occ_energy, wide_index, 1, 0)[0]

    def term(partner, offset, own_slice):
        partner_index = (wide_index + offset) % occ_count
        partner_energy = lax.dynamic_slice_in_dim(occ_energy, partner_index, 1, 0)[0]
        return pair_density(
            own_slice, partner, own_energy, partner_energy, row_energy, vir_energy, kappas
        )

    transformed = jnp.dot(flat_ints, vir_coeff, preferred_element_type=jnp.float32).astype(
        jnp.bfloat16
    )
    transformed = transformed.reshape(aux_local, occ_count, vir_local)
    own_slice = lax.all_to_all(transformed, "wide", split_axis=1, concat_axis=0, tiled=True)[
        :, 0, :
    ]
    own_full = lax.all_gather(own_slice, "batch", axis=1, tiled=True)
    partner = from_behind(own_full, "wide", HALF)
    density = term(partner, -HALF, own_slice)
    for offset in range(1 - HALF, HALF + 1):
        partner = from_behind(partner, "wide", -1)
        density = density + term(partner, offset, own_slice)
    return density.astype(jnp.bfloat16)[:, None, :, :]


def solution(mesh):
    return jax.shard_map(
        on_device,
        mesh=mesh,
        in_specs=(P("wide", None, None), P(None, "batch"), P(), P(), P()),
        out_specs=P(None, "wide", "batch", None),
        check_vma=False,
    )
```

profile of v0, /device:TPU:31, one launch (start us, length us, event | category | flops | bytes accessed | tf_op | source)
XLA Modules:
  0.0 345.7 jit_solution(11318890819423333155)
XLA Ops:
  6.5 0.0 copy-start
  6.5 0.0 all-gather.2.cloned.1.call-start
  6.5 1.5 copy-done
  8.1 1.6 convolution_convert_fusion
  9.7 0.2 reshape.201
  9.9 0.4 copy.16
  10.3 0.2 reshape.207
  10.6 28.0 %all_to_all.15 = bf16[64,2,768]{2,1,0:T(2,128)(2,1)S(1)} all-to-all(bf16[64,2,768]{2,1,0:T(2,128)(2,1)S(1)} %reshape.207), channel_id=1, replica_groups=mesh['wide'=64,'batch'=8] {'wide'}, dimensions={0} | all-to-all | bytes 393216 | tf_op jit(solution)/shard_map/all_to_all | solution.py:48
  38.6 0.3 reshape.208
  38.9 0.8 copy.17
  39.7 0.0 all-gather.2.cloned.1.call-update
  39.7 0.0 copy-start.7
  39.8 0.0 copy-start.6
  39.8 0.0 copy-start.5
  39.8 34.2 %all-gather.2.cloned.1.call-done = bf16[1536,512]{0,1:T(8,128)(2,1)} async-done(((bf16[1536,64]{0,1:T(8,128)(2,1)}), bf16[1536,512]{0,1:T(8,128)(2,1)}) %all-gather.2.cloned.1.call-update) | async-done | bytes 1572880 | tf_op jit(solution)/shard_map/all_gather | solution.py:51
  73.9 2.6 copy.18
  76.5 4.3 %collective-permute-start = (bf16[1536,512]{1,0:T(8,128)(2,1)}, bf16[1536,512]{1,0:T(8,128)(2,1)S(1)}, u32[]{:S(2)}, u32[]{:S(2)}) collective-permute-start(bf16[1536,512]{1,0:T(8,128)(2,1)} %copy.18), channel_id=1, source_target_pairs={{0,16},{8,24},{16,32},{24,40},{32,48},{40,56},{48,64},{56,72},{64,... | collective-permute-start | bytes 4718600 | tf_op jit(solution)/shard_map/ppermute | solution.py:11
  80.9 56.8 %collective-permute-done = bf16[1536,512]{1,0:T(8,128)(2,1)S(1)} collective-permute-done((bf16[1536,512]{1,0:T(8,128)(2,1)}, bf16[1536,512]{1,0:T(8,128)(2,1)S(1)}, u32[]{:S(2)}, u32[]{:S(2)}) %collective-permute-start) | collective-permute-done | bytes 1572896 | tf_op jit(solution)/shard_map/ppermute | solution.py:11
  137.7 9.7 %collective-permute-start.1 = (bf16[1536,512]{1,0:T(8,128)(2,1)S(1)}, bf16[1536,512]{1,0:T(8,128)(2,1)S(1)}, u32[]{:S(2)}, u32[]{:S(2)}) collective-permute-start(bf16[1536,512]{1,0:T(8,128)(2,1)S(1)} %collective-permute-done), channel_id=1, source_target_pairs={{0,504},{8,0},{16,8},{24,16},{32,24},{40,32},{48,40},{56,48},{64,5... | collective-permute-start | bytes 4718600 | tf_op jit(solution)/shard_map/ppermute | solution.py:11
  147.4 61.3 %collective-permute-done.1 = bf16[1536,512]{1,0:T(8,128)(2,1)S(1)} collective-permute-done((bf16[1536,512]{1,0:T(8,128)(2,1)S(1)}, bf16[1536,512]{1,0:T(8,128)(2,1)S(1)}, u32[]{:S(2)}, u32[]{:S(2)}) %collective-permute-start.1) | collective-permute-done | bytes 1572896 | tf_op jit(solution)/shard_map/ppermute | solution.py:11
  208.8 1.2 copy-done.1
  210.0 1.9 collective-permute-start.2
  211.9 51.3 %collective-permute-done.2 = bf16[1536,512]{1,0:T(8,128)(2,1)} collective-permute-done((bf16[1536,512]{1,0:T(8,128)(2,1)S(1)}, bf16[1536,512]{1,0:T(8,128)(2,1)}, u32[]{:S(2)}, u32[]{:S(2)}) %collective-permute-start.2) | collective-permute-done | bytes 1572896 | tf_op jit(solution)/shard_map/ppermute | solution.py:11
  263.2 0.0 copy-done.3
  263.2 1.9 collective-permute-start.3
  265.2 0.0 copy-done.7
  265.2 0.0 copy-done.6
  265.2 0.0 copy-start.4
  265.3 0.1 dynamic_slice.21
  265.3 0.0 copy-done.5
  265.3 0.7 fusion.38
  266.0 3.7 %fusion.28 = (f32[64,512]{1,0:T(8,128)S(1)}, f32[64,512]{1,0:T(8,128)S(1)}, f32[64,512]{1,0:T(8,128)S(1)}, f32[64,512]{1,0:T(8,128)S(1)}, f32[64,512]{1,0:T(8,128)S(1)}) fusion(f32[]{:T(128)} %bitcast.15, f32[]{:T(128)} %bitcast.6, f32[512]{0:T(512)S(1)} %copy-done.6, f32[64]{0:T(128)S(1)} %dynamic_slice.21, f32[]{:T(128)} %bitcast.13, f32[]{:T(128)} %bitcast.11, ...), kind=kLoop, calls=%fused_computation.44 | loop fusion | flops 229376 | bytes 657688 | tf_op jit(solution)/shard_map/sub | solution.py:18
  269.8 1.8 convolution_negate_fusion.4
  271.6 0.0 copy-done.4
  271.6 0.0 copy-start.2
  271.6 1.1 fusion.6
  272.7 0.3 copy-done.2
  273.0 0.4 convolution_negate_fusion.3
  273.4 38.6 %collective-permute-done.3 = bf16[1536,512]{1,0:T(8,128)(2,1)} collective-permute-done((bf16[1536,512]{1,0:T(8,128)(2,1)}, bf16[1536,512]{1,0:T(8,128)(2,1)}, u32[]{:S(2)}, u32[]{:S(2)}) %collective-permute-start.3) | collective-permute-done | bytes 1572896 | tf_op jit(solution)/shard_map/ppermute | solution.py:11
  312.0 1.9 collective-permute-start.4
  313.9 1.1 convolution_add_fusion.3
  315.0 1.8 convolution_negate_fusion.2
  316.8 2.5 convolution_add_fusion.2
  319.3 1.8 convolution_negate_fusion.1
  321.1 2.5 convolution_add_fusion.1
  323.6 12.6 %collective-permute-done.4 = bf16[1536,512]{1,0:T(8,128)(2,1)S(1)} collective-permute-done((bf16[1536,512]{1,0:T(8,128)(2,1)}, bf16[1536,512]{1,0:T(8,128)(2,1)S(1)}, u32[]{:S(2)}, u32[]{:S(2)}) %collective-permute-start.4) | collective-permute-done | bytes 1572896 | tf_op jit(solution)/shard_map/ppermute | solution.py:11
  336.2 0.4 convolution_negate_fusion
  336.6 2.2 fusion.1
  (3 shorter events, 0.0 us)
Async XLA Ops:
  6.5 1.5 copy-start
  6.5 67.4 %all-gather.2.cloned.1.call-start = ((), (), s32[]{:S(2)}) async-start(), calls=%async_computation.1 | async-start | bytes 1769472 | tf_op jit(solution)/shard_map/all_gather | solution.py:51
  39.7 225.4 %copy-start.7 = (f32[8]{0:T(128)S(1)}, f32[8]{0:T(128)}, u32[]{:S(2)}) copy-start(f32[8]{0:T(128)} %param.9) | copy-start | bytes 100
  39.8 225.5 %copy-start.6 = (f32[512]{0:T(512)S(1)}, f32[512]{0:T(512)}, u32[]{:S(2)}) copy-start(f32[512]{0:T(512)} %param.8) | copy-start | bytes 6148
  39.8 225.6 %copy-start.5 = (f32[64]{0:T(128)S(1)}, f32[64]{0:T(128)}, u32[]{:S(2)}) copy-start(f32[64]{0:T(128)} %param.7) | copy-start | bytes 772
  76.5 61.2 %collective-permute-start = (bf16[1536,512]{1,0:T(8,128)(2,1)}, bf16[1536,512]{1,0:T(8,128)(2,1)S(1)}, u32[]{:S(2)}, u32[]{:S(2)}) collective-permute-start(bf16[1536,512]{1,0:T(8,128)(2,1)} %copy.18), channel_id=1, source_target_pairs={{0,16},{8,24},{16,32},{24,40},{32,48},{40,56},{48,64},{56,72},{64,... | collective-permute-start | bytes 4718600 | tf_op jit(solution)/shard_map/ppermute | solution.py:11
  137.7 125.5 %copy-start.3 = (bf16[1536,512]{1,0:T(8,128)(2,1)}, bf16[1536,512]{1,0:T(8,128)(2,1)S(1)}, u32[]{:S(2)}) copy-start(bf16[1536,512]{1,0:T(8,128)(2,1)S(1)} %collective-permute-done) | copy-start | bytes 4718596
  137.7 71.1 %collective-permute-start.1 = (bf16[1536,512]{1,0:T(8,128)(2,1)S(1)}, bf16[1536,512]{1,0:T(8,128)(2,1)S(1)}, u32[]{:S(2)}, u32[]{:S(2)}) collective-permute-start(bf16[1536,512]{1,0:T(8,128)(2,1)S(1)} %collective-permute-done), channel_id=1, source_target_pairs={{0,504},{8,0},{16,8},{24,16},{32,24},{40,32},{48,40},{56,48},{64,5... | collective-permute-start | bytes 4718600 | tf_op jit(solution)/shard_map/ppermute | solution.py:11
  208.8 1.2 copy-start.1
  210.0 53.2 %collective-permute-start.2 = (bf16[1536,512]{1,0:T(8,128)(2,1)S(1)}, bf16[1536,512]{1,0:T(8,128)(2,1)}, u32[]{:S(2)}, u32[]{:S(2)}) collective-permute-start(bf16[1536,512]{1,0:T(8,128)(2,1)S(1)} %collective-permute-done.1), channel_id=1, source_target_pairs={{0,504},{8,0},{16,8},{24,16},{32,24},{40,32},{48,40},{56,48},{64,5... | collective-permute-start | bytes 4718600 | tf_op jit(solution)/shard_map/ppermute | solution.py:11
  263.2 48.8 %collective-permute-start.3 = (bf16[1536,512]{1,0:T(8,128)(2,1)}, bf16[1536,512]{1,0:T(8,128)(2,1)}, u32[]{:S(2)}, u32[]{:S(2)}) collective-permute-start(bf16[1536,512]{1,0:T(8,128)(2,1)} %collective-permute-done.2), channel_id=1, source_target_pairs={{0,504},{8,0},{16,8},{24,16},{32,24},{40,32},{48,40},{56,48},{64,5... | collective-permute-start | bytes 4718600 | tf_op jit(solution)/shard_map/ppermute | solution.py:11
  265.2 6.3 %copy-start.4 = (bf16[1536,512]{1,0:T(8,128)(2,1)S(1)}, bf16[1536,512]{1,0:T(8,128)(2,1)}, u32[]{:S(2)}) copy-start(bf16[1536,512]{1,0:T(8,128)(2,1)} %copy-done.3) | copy-start | bytes 4718596
  271.6 1.4 copy-start.2
  312.0 24.2 %collective-permute-start.4 = (bf16[1536,512]{1,0:T(8,128)(2,1)}, bf16[1536,512]{1,0:T(8,128)(2,1)S(1)}, u32[]{:S(2)}, u32[]{:S(2)}) collective-permute-start(bf16[1536,512]{1,0:T(8,128)(2,1)} %collective-permute-done.3), channel_id=1, source_target_pairs={{0,504},{8,0},{16,8},{24,16},{32,24},{40,32},{48,40},{56,48},{64,5... | collective-permute-start | bytes 4718600 | tf_op jit(solution)/shard_map/ppermute | solution.py:11
Sparse Core Ops, SparseCore 0:
  39.9 34.0 all-gather.1
where the time goes:
time: 346 us
  waiting for transfers between devices  255 us (74%)
  blocking collectives  28 us (8%)
  starting transfers between devices  19.8 us (6%)
  matrix products  17.2 us (5%)
  between operations  13.7 us (4%)
  local copies, waits for them, and re-layouts  8.39 us (2%)
  other arithmetic  3.73 us (1%)
    ppermute x5, waiting for transfers between devices, from_behind(): lax.ppermute(shard, axis, [(i, (i + by) % peers) for i in range(peers)])  221 us
    all_gather x1, waiting for transfers between devices, on_device(): own_full = lax.all_gather(own_slice, 'batch', axis=1, tiled=True)  34.2 us
    all_to_all x1, blocking collectives, on_device(): lax.all_to_all(transformed, 'wide', split_axis=1, concat_axis=0, tiled=True)  28 us
    ppermute x5, starting transfers between devices, from_behind(): lax.ppermute(shard, axis, [(i, (i + by) % peers) for i in range(peers)])  19.8 us
    dot_general x5, matrix products, pair_density(): lax.dot_general(flat, partner, (((1,), (1,)), ((), ())), preferred_elemen...  9.32 us
  transfers between devices with their start and end apart: 6, of which 6 were waited for; matrix products, arithmetic and copies ran while one was open for 5% of the time, Pallas kernels for 0%

commit v1 on v0

--- a/solution.py
+++ b/solution.py
@@ -48,7 +48,9 @@
     own_slice = lax.all_to_all(transformed, "wide", split_axis=1, concat_axis=0, tiled=True)[
         :, 0, :
     ]
-    own_full = lax.all_gather(own_slice, "batch", axis=1, tiled=True)
+    own_full = jnp.concatenate(
+        lax.all_to_all(jnp.stack([own_slice] * lax.axis_size("batch")), "batch", 0, 0), axis=1
+    )
     partner = from_behind(own_full, "wide", HALF)
     density = term(partner, -HALF, own_slice)
     for offset in range(1 - HALF, HALF + 1):

time: 346 us -> 314 us (0.908)
  the two profiles are of different devices: /device:TPU:31 before, /device:TPU:57 now
where the time goes in v1:
time: 314 us
  waiting for transfers between devices  218 us (69%)
  blocking collectives  51.4 us (16%)
  matrix products  17.2 us (5%)
  starting transfers between devices  15.3 us (5%)
  local copies, waits for them, and re-layouts  7.87 us (3%)
  other arithmetic  3.79 us (1%)
    ppermute x5, waiting for transfers between devices, from_behind(): lax.ppermute(shard, axis, [(i, (i + by) % peers) for i in range(peers)])  218 us
    all_to_all x1, blocking collectives, on_device(): lax.all_to_all(transformed, 'wide', split_axis=1, concat_axis=0, tiled=True)  27.3 us
    all_to_all x1, blocking collectives, on_device(): lax.all_to_all(jnp.stack([own_slice] * lax.axis_size('batch')), 'batch',...  24.1 us
    ppermute x5, starting transfers between devices, from_behind(): lax.ppermute(shard, axis, [(i, (i + by) % peers) for i in range(peers)])  15.3 us
    dot_general x5, matrix products, pair_density(): lax.dot_general(flat, partner, (((1,), (1,)), ((), ())), preferred_elemen...  9.31 us
  transfers between devices with their start and end apart: 5, of which 5 were waited for; matrix products, arithmetic and copies ran while one was open for 6% of the time, Pallas kernels for 0%

profile of v1, /device:TPU:57, one launch (start us, length us, event | category | flops | bytes accessed | tf_op | source)
XLA Modules:
  0.0 313.8 jit_solution(3556500056317765634)
XLA Ops:
  0.0 0.0 copy-start
  0.0 1.5 copy-done
  1.5 1.6 convolution_convert_fusion
  3.2 0.2 reshape.210
  3.4 0.4 copy.7
  3.8 0.2 reshape.218
  4.0 27.3 %all_to_all.20 = bf16[64,2,768]{2,1,0:T(2,128)(2,1)S(1)} all-to-all(bf16[64,2,768]{2,1,0:T(2,128)(2,1)S(1)} %reshape.218), channel_id=1, replica_groups=mesh['wide'=64,'batch'=8] {'wide'}, dimensions={0} | all-to-all | bytes 393216 | tf_op jit(solution)/shard_map/all_to_all | solution.py:48
  31.3 0.3 reshape.219
  31.6 0.2 copy.8
  31.8 0.1 stack.3
  31.9 24.1 %all_to_all.21 = bf16[8,1536,64]{1,2,0:T(8,128)(2,1)} all-to-all(bf16[8,1536,64]{1,2,0:T(8,128)(2,1)S(1)} %stack.3), channel_id=1, replica_groups=mesh['wide'=64,'batch'=8] {'batch'}, dimensions={0} | all-to-all | bytes 3145728 | tf_op jit(solution)/shard_map/all_to_all | solution.py:52
  56.0 0.0 copy-start.7
  56.0 0.0 copy-start.6
  56.0 0.0 copy-start.5
  56.0 2.6 copy.9
  58.6 1.9 collective-permute-start
  60.5 62.7 %collective-permute-done = bf16[1536,512]{1,0:T(8,128)(2,1)S(1)} collective-permute-done((bf16[1536,512]{1,0:T(8,128)(2,1)}, bf16[1536,512]{1,0:T(8,128)(2,1)S(1)}, u32[]{:S(2)}, u32[]{:S(2)}) %collective-permute-start) | collective-permute-done | bytes 1572896 | tf_op jit(solution)/shard_map/ppermute | solution.py:11
  123.2 0.0 copy-start.3
  123.2 7.7 %collective-permute-start.1 = (bf16[1536,512]{1,0:T(8,128)(2,1)S(1)}, bf16[1536,512]{1,0:T(8,128)(2,1)S(1)}, u32[]{:S(2)}, u32[]{:S(2)}) collective-permute-start(bf16[1536,512]{1,0:T(8,128)(2,1)S(1)} %collective-permute-done), channel_id=1, source_target_pairs={{0,504},{8,0},{16,8},{24,16},{32,24},{40,32},{48,40},{56,48},{64,5... | collective-permute-start | bytes 4718600 | tf_op jit(solution)/shard_map/ppermute | solution.py:11
  130.9 38.2 %collective-permute-done.1 = bf16[1536,512]{1,0:T(8,128)(2,1)S(1)} collective-permute-done((bf16[1536,512]{1,0:T(8,128)(2,1)S(1)}, bf16[1536,512]{1,0:T(8,128)(2,1)S(1)}, u32[]{:S(2)}, u32[]{:S(2)}) %collective-permute-start.1) | collective-permute-done | bytes 1572896 | tf_op jit(solution)/shard_map/ppermute | solution.py:11
  169.1 1.2 copy-done.1
  170.3 1.9 collective-permute-start.2
  172.2 61.3 %collective-permute-done.2 = bf16[1536,512]{1,0:T(8,128)(2,1)} collective-permute-done((bf16[1536,512]{1,0:T(8,128)(2,1)S(1)}, bf16[1536,512]{1,0:T(8,128)(2,1)}, u32[]{:S(2)}, u32[]{:S(2)}) %collective-permute-start.2) | collective-permute-done | bytes 1572896 | tf_op jit(solution)/shard_map/ppermute | solution.py:11
  233.4 0.0 copy-done.3
  233.4 1.9 collective-permute-start.3
  235.4 0.0 copy-done.7
  235.5 0.0 copy-done.6
  235.5 0.0 copy-start.4
  235.5 0.1 dynamic_slice.21
  235.6 0.0 copy-done.5
  235.6 0.7 fusion.38
  236.3 3.8 %fusion.28 = (f32[64,512]{1,0:T(8,128)S(1)}, f32[64,512]{1,0:T(8,128)S(1)}, f32[64,512]{1,0:T(8,128)S(1)}, f32[64,512]{1,0:T(8,128)S(1)}, f32[64,512]{1,0:T(8,128)S(1)}) fusion(f32[]{:T(128)} %bitcast.17, f32[]{:T(128)} %bitcast.8, f32[512]{0:T(512)S(1)} %copy-done.6, f32[64]{0:T(128)S(1)} %dynamic_slice.21, f32[]{:T(128)} %bitcast.15, f32[]{:T(128)} %bitcast.13, ...), kind=kLoop, calls=%fused_computation.44 | loop fusion | flops 229376 | bytes 657688 | tf_op jit(solution)/shard_map/sub | solution.py:18
  240.1 1.8 convolution_negate_fusion.4
  241.9 0.0 copy-done.4
  241.9 0.0 copy-start.2
  241.9 1.1 fusion.6
  243.0 0.3 copy-done.2
  243.3 0.4 convolution_negate_fusion.3
  243.7 34.9 %collective-permute-done.3 = bf16[1536,512]{1,0:T(8,128)(2,1)} collective-permute-done((bf16[1536,512]{1,0:T(8,128)(2,1)}, bf16[1536,512]{1,0:T(8,128)(2,1)}, u32[]{:S(2)}, u32[]{:S(2)}) %collective-permute-start.3) | collective-permute-done | bytes 1572896 | tf_op jit(solution)/shard_map/ppermute | solution.py:11
  278.6 1.9 collective-permute-start.4
  280.5 1.1 convolution_add_fusion.3
  281.6 1.8 convolution_negate_fusion.2
  283.4 2.5 convolution_add_fusion.2
  285.9 1.8 convolution_negate_fusion.1
  287.8 2.5 convolution_add_fusion.1
  290.3 21.0 %collective-permute-done.4 = bf16[1536,512]{1,0:T(8,128)(2,1)S(1)} collective-permute-done((bf16[1536,512]{1,0:T(8,128)(2,1)}, bf16[1536,512]{1,0:T(8,128)(2,1)S(1)}, u32[]{:S(2)}, u32[]{:S(2)}) %collective-permute-start.4) | collective-permute-done | bytes 1572896 | tf_op jit(solution)/shard_map/ppermute | solution.py:11
  311.2 0.4 convolution_negate_fusion
  311.6 2.2 fusion.1
  (2 shorter events, 0.0 us)
Async XLA Ops:
  0.0 1.5 copy-start
  56.0 179.5 %copy-start.7 = (f32[8]{0:T(128)S(1)}, f32[8]{0:T(128)}, u32[]{:S(2)}) copy-start(f32[8]{0:T(128)} %param.9) | copy-start | bytes 100
  56.0 179.5 %copy-start.6 = (f32[512]{0:T(512)S(1)}, f32[512]{0:T(512)}, u32[]{:S(2)}) copy-start(f32[512]{0:T(512)} %param.8) | copy-start | bytes 6148
  56.0 179.6 %copy-start.5 = (f32[64]{0:T(128)S(1)}, f32[64]{0:T(128)}, u32[]{:S(2)}) copy-start(f32[64]{0:T(128)} %param.7) | copy-start | bytes 772
  58.6 64.6 %collective-permute-start = (bf16[1536,512]{1,0:T(8,128)(2,1)}, bf16[1536,512]{1,0:T(8,128)(2,1)S(1)}, u32[]{:S(2)}, u32[]{:S(2)}) collective-permute-start(bf16[1536,512]{1,0:T(8,128)(2,1)} %copy.9), channel_id=1, source_target_pairs={{0,16},{8,24},{16,32},{24,40},{32,48},{40,56},{48,64},{56,72},{64,... | collective-permute-start | bytes 4718600 | tf_op jit(solution)/shard_map/ppermute | solution.py:11
  123.2 110.2 %copy-start.3 = (bf16[1536,512]{1,0:T(8,128)(2,1)}, bf16[1536,512]{1,0:T(8,128)(2,1)S(1)}, u32[]{:S(2)}) copy-start(bf16[1536,512]{1,0:T(8,128)(2,1)S(1)} %collective-permute-done) | copy-start | bytes 4718596
  123.2 45.8 %collective-permute-start.1 = (bf16[1536,512]{1,0:T(8,128)(2,1)S(1)}, bf16[1536,512]{1,0:T(8,128)(2,1)S(1)}, u32[]{:S(2)}, u32[]{:S(2)}) collective-permute-start(bf16[1536,512]{1,0:T(8,128)(2,1)S(1)} %collective-permute-done), channel_id=1, source_target_pairs={{0,504},{8,0},{16,8},{24,16},{32,24},{40,32},{48,40},{56,48},{64,5... | collective-permute-start | bytes 4718600 | tf_op jit(solution)/shard_map/ppermute | solution.py:11
  169.1 1.2 copy-start.1
  170.3 63.2 %collective-permute-start.2 = (bf16[1536,512]{1,0:T(8,128)(2,1)S(1)}, bf16[1536,512]{1,0:T(8,128)(2,1)}, u32[]{:S(2)}, u32[]{:S(2)}) collective-permute-start(bf16[1536,512]{1,0:T(8,128)(2,1)S(1)} %collective-permute-done.1), channel_id=1, source_target_pairs={{0,504},{8,0},{16,8},{24,16},{32,24},{40,32},{48,40},{56,48},{64,5... | collective-permute-start | bytes 4718600 | tf_op jit(solution)/shard_map/ppermute | solution.py:11
  233.4 45.2 %collective-permute-start.3 = (bf16[1536,512]{1,0:T(8,128)(2,1)}, bf16[1536,512]{1,0:T(8,128)(2,1)}, u32[]{:S(2)}, u32[]{:S(2)}) collective-permute-start(bf16[1536,512]{1,0:T(8,128)(2,1)} %collective-permute-done.2), channel_id=1, source_target_pairs={{0,504},{8,0},{16,8},{24,16},{32,24},{40,32},{48,40},{56,48},{64,5... | collective-permute-start | bytes 4718600 | tf_op jit(solution)/shard_map/ppermute | solution.py:11
  235.5 6.4 %copy-start.4 = (bf16[1536,512]{1,0:T(8,128)(2,1)S(1)}, bf16[1536,512]{1,0:T(8,128)(2,1)}, u32[]{:S(2)}) copy-start(bf16[1536,512]{1,0:T(8,128)(2,1)} %copy-done.3) | copy-start | bytes 4718596
  241.9 1.4 copy-start.2
  278.6 32.6 %collective-permute-start.4 = (bf16[1536,512]{1,0:T(8,128)(2,1)}, bf16[1536,512]{1,0:T(8,128)(2,1)S(1)}, u32[]{:S(2)}, u32[]{:S(2)}) collective-permute-start(bf16[1536,512]{1,0:T(8,128)(2,1)} %collective-permute-done.3), channel_id=1, source_target_pairs={{0,504},{8,0},{16,8},{24,16},{32,24},{40,32},{48,40},{56,48},{64,5... | collective-permute-start | bytes 4718600 | tf_op jit(solution)/shard_map/ppermute | solution.py:11
